TPU v7x, 32 devices: a whole 2x2x4 slice. The times are simulated.
32 devices in a mesh: gx: 8 (over y, x, core), gy: 4 (over z).
Axes of the slice: x: 2, y: 2, z: 4, core: 2. Of those that a mesh axis runs over, the one named last changes fastest.
Arguments:
- displacement: float32 [3, 24, 32, 128], P(None, 'gx', 'gy'), may hold values from -0.1 to 0.1
- velocity: float32 [3, 24, 32, 128], P(None, 'gx', 'gy'), may hold values from -0.6 to 0.6
- bone: int32 [24, 32, 128], P('gx', 'gy'), may hold values 0 or 1
- broken: int32 [4, 24, 32, 128], P(None, 'gx', 'gy'), may hold values from 0 to 65535, as said below
Outputs:
- velocity_end: float32 [3, 24, 32, 128], P(None, 'gx', 'gy')
- damage: float32 [24, 32, 128], P('gx', 'gy')
Inputs may be any that keep to these rules, and one draw needn't show every extreme that they name: 1 marks bone, 0 void. `broken`: only the bits that flag bonds are used: bits 0 to 15 of word 0 and bits 0 to 14 of words 1 to 3.
All inputs are finite; a program needn't handle non-finite values. No bound on the sum of `bone` on one device may be relied on, other than what follows from the above.
Results may differ from a plain program's by a relative error of at most 0.000069.
Values sent between devices are 32-bit elements; how exact they have to be, the bound alone decides.
A program may use at most 128 MiB of HBM per device.

v0:
```python
import functools
import math

import jax
import jax.numpy as jnp
from jax import lax
from jax.experimental import pallas as pl
from jax.experimental.pallas import tpu as pltpu
from jax.sharding import PartitionSpec as P

STEPS = 2
REACH = 3

BULK_TERM = -50.0
SHEAR_TERM = 1500.0
TIME_STEP = 0.1
STRETCH_CRITICAL = 0.04
STRETCH_WIDTH = 0.01
DIRECTION_EPS = 1e-06
LOG2_E = math.log2(math.e)

ROW = 4

AROUND = [(dx, dy) for dx in (-1, 0, 1) for dy in (-1, 0, 1) if (dx, dy) != (0, 0)]


def half_bonds():
    listed = []
    for step_x in range(0, 4):
        for step_y in range(-3, 4):
            for step_z in range(-3, 4):
                forward_half = step_x > 0 or (
                    step_x == 0 and (step_y > 0 or (step_y == 0 and step_z > 0))
                )
                if forward_half and step_x * step_x + step_y * step_y + step_z * step_z <= 9:
                    listed.append((step_x, step_y, step_z))
    return listed


def flag_place(number):
    if number < 16:
        return (0, number)
    return (1 + (number - 16) // 15, (number - 16) % 15)


def every_bond():
    listed = []
    for number, (step_x, step_y, step_z) in enumerate(half_bonds()):
        listed.append((step_x, step_y, step_z, number, False))
        listed.append((-step_x, -step_y, -step_z, number, True))
    return listed


def packed_rows(fields, layers):
    return -(-fields * layers * REACH // 8) * 8


class Exchange:
    def __init__(self, own, packed, from_x, from_y, send_sem, recv_sem, base, sides, place, has):
        self.own, self.packed = own, packed
        self.from_x, self.from_y = from_x, from_y
        self.send_sem, self.recv_sem, self.base = send_sem, recv_sem, base
        self.sides, self.place, self.has = sides, place, has
        self.low_dx = min(-dx for dx, dy in sides)

    def copy(self, number):
        dx, dy = self.sides[number]
        if dy == 0:
            source = self.own
            target = self.from_x.at[0 if dx == 1 else 1]
        else:
            source = self.packed.at[0 if dy == -1 else 1]
            target = self.from_y.at[-dx - self.low_dx, 0 if dy == 1 else 1]
        return pltpu.make_async_remote_copy(
            src_ref=source,
            dst_ref=target,
            send_sem=self.send_sem.at[self.base + number],
            recv_sem=self.recv_sem.at[self.base + number],
            device_id={"gx": self.place[0] + dx, "gy": self.place[1] + dy},
            device_id_type=pl.DeviceIdType.MESH,
        )

    def pack(self):
        fields, layers, rows = self.own.shape[:3]
        for field in range(fields):
            for layer in range(layers):
                at = (field * layers + layer) * REACH
                self.packed[0, at : at + REACH] = self.own[field, layer, 0:REACH]
                self.packed[1, at : at + REACH] = self.own[field, layer, rows - REACH : rows]

    def clear(self):
        for dx, dy in self.sides:
            if dy == 0:
                slot = self.from_x.at[0 if dx == 1 else 1]
            else:
                slot = self.from_y.at[-dx - self.low_dx, 0 if dy == 1 else 1]

            @pl.when(jnp.logical_not(self.has(-dx, -dy)))
            def _():
                slot[...] = jnp.zeros(slot.shape, slot.dtype)

    def start(self):
        for number, (dx, dy) in enumerate(self.sides):

            @pl.when(self.has(dx, dy))
            def _():
                self.copy(number).start()

    def wait_recv(self):
        for number, (dx, dy) in enumerate(self.sides):

            @pl.when(self.has(-dx, -dy))
            def _():
                self.copy(number).wait_recv()

    def wait_send(self):
        for number, (dx, dy) in enumerate(self.sides):

            @pl.when(self.has(dx, dy))
            def _():
                self.copy(number).wait_send()

    def assemble(self, extended, dxs):
        fields, layers, rows = self.own.shape[:3]
        for dx in dxs:
            for field in range(fields):
                for layer in range(layers):
                    whole = (dx + 1) * layers + layer
                    at = (field * layers + layer) * REACH
                    if dx == 0:
                        tile = self.own[field, layer]
                    else:
                        tile = self.from_x[0 if dx == -1 else 1, field, layer]
                    y_at = dx - self.low_dx
                    extended[field, whole, ROW : ROW + rows] = tile
                    extended[field, whole, ROW - REACH : ROW] = self.from_y[y_at, 0, at : at + REACH]
                    extended[field, whole, ROW + rows : ROW + rows + REACH] = self.from_y[
                        y_at, 1, at : at + REACH
                    ]


def spread_rolls(rolled, fields, change=None):
    layers, rows, depth = rolled.shape[2:]

    @pl.loop(0, layers)
    def _(layer):
        for field in fields:
            for half in range(0, rows, 8):
                tile = rolled[REACH, field, layer, half : half + 8]
                for step_z in range(-REACH, REACH + 1):
                    if step_z == 0:
                        continue
                    moved = pltpu.roll(tile, (-step_z) % depth, 1)
                    if change is not None:
                        moved = change(moved, field, step_z)
                    rolled[REACH + step_z, field, layer, half : half + 8] = moved


def kernel(
    count_x, count_y,
    u_ref, v_ref, bone_ref, words_ref,
    velocity_ref, damage_ref,
    own1, pack1, fx1, fy1,
    packw, fxw, fyw,
    own2, pack2, fx2, fy2,
    own3, pack3, fx3, fy3,
    own4, pack4, fx4, fy4,
    near, near_words, ratio, masks, pulls, stretches, volumes,
    send_sem, recv_sem,
):
    place = (lax.axis_index("gx"), lax.axis_index("gy"))
    layers, rows, depth = bone_ref.shape
    bonds = every_bond()

    def has(dx, dy):
        there = None
        for at, step, count in ((place[0], dx, count_x), (place[1], dy, count_y)):
            if step == 0:
                continue
            good = at > 0 if step < 0 else at < count - 1
            there = good if there is None else jnp.logical_and(there, good)
        return there

    def exchange(own, packed, from_x, from_y, base, sides):
        return Exchange(own, packed, from_x, from_y, send_sem, recv_sem, base, sides, place, has)

    word_sides = [(dx, dy) for dx, dy in AROUND if dx >= 0]
    count = len(AROUND)
    first = exchange(own1, pack1, fx1, fy1, 0, AROUND)
    flags = exchange(words_ref, packw, fxw, fyw, count, word_sides)
    base = count + len(word_sides)
    second = exchange(own2, pack2, fx2, fy2, base, AROUND)
    third = exchange(own3, pack3, fx3, fy3, base + count, AROUND)
    fourth = exchange(own4, pack4, fx4, fy4, base + 2 * count, AROUND)
    exchanges = (first, flags, second, third, fourth)

    barrier = pltpu.get_barrier_semaphore()
    expected = jnp.int32(0)
    for dx, dy in AROUND:
        there = has(dx, dy)
        expected = expected + there.astype(jnp.int32)

        @pl.when(there)
        def _():
            pl.semaphore_signal(
                barrier,
                inc=1,
                device_id={"gx": place[0] + dx, "gy": place[1] + dy},
                device_id_type=pl.DeviceIdType.MESH,
            )

    for part in exchanges:
        part.packed[...] = jnp.zeros(part.packed.shape, part.packed.dtype)
        part.clear()
    for axis in range(3):
        own1[axis] = u_ref[axis]
    own1[3] = bone_ref[...].astype(jnp.float32)
    first.pack()
    flags.pack()
    pl.semaphore_wait(barrier, expected)
    first.start()
    flags.start()

    lane = lax.broadcasted_iota(jnp.int32, (8, depth), 1)

    def shifted(moved, field, step_z):
        if field == 2:
            return moved + float(step_z)
        if field == 3:
            inside = (lane + step_z >= 0) & (lane + step_z < depth)
            return jnp.where(inside, moved, 0.0)
        return moved

    for step_index in range(STEPS):
        opening = step_index == 0
        last_step = step_index == STEPS - 1
        source = first if opening else third
        source.wait_recv()
        source.assemble(near.at[REACH], (-1, 0, 1))
        spread_rolls(near, range(4 if opening else 3), shifted)
        if opening:
            flags.wait_recv()
            flags.assemble(near_words.at[REACH], (-1, 0))
            spread_rolls(near_words, range(4))
        moving = u_ref if opening else own3
        ratios = second if opening else fourth

        @pl.loop(0, layers)
        def _(layer):
            here = [moving[axis, layer] for axis in range(3)]
            total = jnp.zeros((rows, depth), jnp.float32)
            sums = {}
            if opening:
                words_here = [words_ref[word, layer] for word in range(4)]
            for number, (step_x, step_y, step_z, flag, backward) in enumerate(bonds):
                low = ROW + step_y
                rel = []
                for axis, step in enumerate((step_x, step_y, 0)):
                    far = near[REACH + step_z, axis, layer + layers + step_x, low : low + rows]
                    rel.append(far - (here[axis] - float(step)))
                squared = rel[0] * rel[0] + rel[1] * rel[1] + rel[2] * rel[2]
                length = squared * lax.rsqrt(jnp.maximum(squared, 1e-30))
                norm = step_x * step_x + step_y * step_y + step_z * step_z
                natural = math.sqrt(norm)
                extension = length - natural
                power = extension * (LOG2_E / (STRETCH_WIDTH * natural)) - (
                    STRETCH_CRITICAL * LOG2_E / STRETCH_WIDTH
                )
                if opening:
                    word, bit = flag_place(flag)
                    if backward:
                        held = near_words[
                            REACH + step_z, word, layer + layers + step_x, low : low + rows
                        ]
                    else:
                        held = words_here[word]
                    far_bone = near[REACH + step_z, 3, layer + layers + step_x, low : low + rows]
                    intact = jnp.where((held & (1 << bit)) == 0, far_bone, 0.0)
                    masks[number, layer] = intact
                    sums[norm] = sums[norm] + intact if norm in sums else intact
                else:
                    intact = masks[number, layer]
                weight = intact / (1.0 + jnp.exp2(power))
                if last_step:
                    sums[norm] = sums[norm] + weight if norm in sums else weight
                total = total + weight * extension
                stretches[number, layer] = extension * (1.0 / natural)
                pull = weight * lax.rsqrt(squared + DIRECTION_EPS)
                for axis in range(3):
                    pulls[number, axis, layer] = pull * rel[axis]
            bone_here = own1[3, layer]
            weighted = jnp.zeros((rows, depth), jnp.float32)
            for norm, value in sums.items():
                weighted = weighted + value * math.sqrt(norm)
            weighted = weighted * bone_here
            if opening:
                volume = jnp.maximum(weighted, 1.0)
                inverse = 1.0 / volume
                volumes[layer] = inverse
                own2[1, layer] = inverse * SHEAR_TERM
            else:
                inverse = volumes[layer]
            if last_step:
                damage_ref[layer] = 1.0 - weighted * inverse
            scaled = (3.0 * (total * bone_here) * inverse) * inverse
            ratios.own[0, layer] = scaled * BULK_TERM

        ratios.pack()
        ratios.start()
        ratios.wait_recv()
        ratios.assemble(ratio.at[REACH], (-1, 0, 1))
        spread_rolls(ratio, range(2 if opening else 1))

        @pl.loop(0, layers)
        def _(layer):
            scaled = ratios.own[0, layer]
            inverse = own2[1, layer]
            force = [jnp.zeros((rows, depth), jnp.float32) for axis in range(3)]
            for number, (step_x, step_y, step_z, flag, backward) in enumerate(bonds):
                low = ROW + step_y
                far = [
                    ratio[REACH + step_z, kind, layer + layers + step_x, low : low + rows]
                    for kind in range(2)
                ]
                magnitude = (scaled + far[0]) + stretches[number, layer] * (inverse + far[1])
                for axis in range(3):
                    force[axis] = force[axis] + magnitude * pulls[number, axis, layer]
            bone_here = own1[3, layer] * TIME_STEP
            for axis in range(3):
                before = v_ref[axis, layer] if opening else velocity_ref[axis, layer]
                speed = before + force[axis] * bone_here
                velocity_ref[axis, layer] = speed
                if not last_step:
                    own3[axis, layer] = u_ref[axis, layer] + TIME_STEP * speed

        if not last_step:
            third.pack()
            third.start()

    for part in exchanges:
        part.wait_send()


def body(count_x, count_y, displacement, velocity, bone, broken):
    layers, rows, depth = bone.shape
    bonds = len(every_bond())

    def floats(*shape):
        return pltpu.VMEM(shape, jnp.float32)

    def exchanged(fields):
        packed = packed_rows(fields, layers)
        return [
            floats(fields, layers, rows, depth),
            floats(2, packed, depth),
            floats(2, fields, layers, rows, depth),
            floats(3, 2, packed, depth),
        ]

    words = broken.shape[0]
    packed = packed_rows(words, layers)
    tall = rows + 8
    copies = 4 * len(AROUND) + 5
    scratch = (
        exchanged(4)
        + [
            pltpu.VMEM((2, packed, depth), jnp.int32),
            pltpu.VMEM((1, words, layers, rows, depth), jnp.int32),
            pltpu.VMEM((2, 2, packed, depth), jnp.int32),
        ]
        + exchanged(2)
        + exchanged(3)
        + exchanged(1)
        + [
            floats(2 * REACH + 1, 4, 3 * layers, tall, depth),
            pltpu.VMEM((2 * REACH + 1, words, 2 * layers, tall, depth), jnp.int32),
            floats(2 * REACH + 1, 2, 3 * layers, tall, depth),
            floats(bonds, layers, rows, depth),
            floats(bonds, 3, layers, rows, depth),
            floats(bonds, layers, rows, depth),
            floats(layers, rows, depth),
            pltpu.SemaphoreType.DMA((copies,)),
            pltpu.SemaphoreType.DMA((copies,)),
        ]
    )
    vmem = pl.BlockSpec(memory_space=pltpu.VMEM)
    return pl.pallas_call(
        functools.partial(kernel, count_x, count_y),
        out_shape=(
            jax.ShapeDtypeStruct(velocity.shape, jnp.float32),
            jax.ShapeDtypeStruct(bone.shape, jnp.float32),
        ),
        in_specs=[vmem] * 4,
        out_specs=(vmem, vmem),
        scratch_shapes=scratch,
        compiler_params=pltpu.CompilerParams(collective_id=0, has_side_effects=True),
    )(displacement, velocity, bone, broken)


def solution(mesh):
    in_specs = (
        P(None, "gx", "gy", None),
        P(None, "gx", "gy", None),
        P("gx", "gy", None),
        P(None, "gx", "gy", None),
    )
    out_specs = (P(None, "gx", "gy", None), P("gx", "gy", None))
    run = functools.partial(body, mesh.shape["gx"], mesh.shape["gy"])
    return jax.shard_map(run, mesh=mesh, in_specs=in_specs, out_specs=out_specs, check_vma=False)
```

profile of v0, /device:TPU:3, one launch (start us, length us, event | category | flops | bytes accessed | tf_op | source)
XLA Modules:
  0.0 32.5 jit_solution(7234957025823683008)
XLA Ops:
  0.6 29.8 %shard_map.59 = (f32[3,3,8,128]{3,2,1,0:T(8,128)}, f32[3,8,128]{2,1,0:T(8,128)}) custom-call(f32[3,3,8,128]{3,2,1,0:T(8,128)} %u_ref.1, f32[3,3,8,128]{3,2,1,0:T(8,128)} %v_ref.1, s32[3,8,128]{2,1,0:T(8,128)} %bone_ref.1, s32[4,3,8,128]{3,2,1,0:T(8,128)} %words_ref.1), custom_call_target="tpu_custom_call" | custom-call | tf_op jit(solution)/shard_map/pallas_call | solution.py:387
  30.5 0.0 copy-start
  30.5 1.4 %copy.8 = f32[3,3,8,128]{3,2,1,0:T(8,128)} copy(f32[3,3,8,128]{3,2,1,0:T(8,128)} %get-tuple-element.4) | data formatting | bytes 73728
  31.9 0.0 copy-done
  31.9 0.6 %copy.9 = f32[3,8,128]{2,1,0:T(8,128)} copy(f32[3,8,128]{2,1,0:T(8,128)S(1)} %copy-done) | data formatting | bytes 24576
Async XLA Ops:
  30.5 1.4 %copy-start = (f32[3,8,128]{2,1,0:T(8,128)S(1)}, f32[3,8,128]{2,1,0:T(8,128)}, u32[]{:S(2)}) copy-start(f32[3,8,128]{2,1,0:T(8,128)} %get-tuple-element.5) | copy-start | bytes 36868
where the time goes:
time: 32.7 us; the launch traced here: 32.5 us
  Pallas kernels  29.8 us (91%)
  local copies, waits for them, and re-layouts  2 us (6%)
  between operations  0.65 us (2%)
    pallas_call x1, Pallas kernels, body(): pl.pallas_call(functools.partial(kernel, count_x, count_y), out_shape=(ja...  29.8 us
    unnamed x4, local copies, waits for them, and re-layouts  2 us

commit v1 on v0

--- a/solution.py
+++ b/solution.py
@@ -10,6 +10,7 @@
 
 STEPS = 2
 REACH = 3
+VMEM_BYTES = 60 * 1024 * 1024
 
 BULK_TERM = -50.0
 SHEAR_TERM = 1500.0
@@ -158,15 +159,16 @@
 
 def kernel(
     count_x, count_y,
+    u_hbm, v_hbm, bone_hbm, words_hbm,
+    velocity_ref, damage_ref,
     u_ref, v_ref, bone_ref, words_ref,
-    velocity_ref, damage_ref,
     own1, pack1, fx1, fy1,
     packw, fxw, fyw,
     own2, pack2, fx2, fy2,
     own3, pack3, fx3, fy3,
     own4, pack4, fx4, fy4,
     near, near_words, ratio, masks, pulls, stretches, volumes,
-    send_sem, recv_sem,
+    send_sem, recv_sem, load_sem,
 ):
     place = (lax.axis_index("gx"), lax.axis_index("gy"))
     layers, rows, depth = bone_ref.shape
@@ -194,6 +196,14 @@
     fourth = exchange(own4, pack4, fx4, fy4, base + 2 * count, AROUND)
     exchanges = (first, flags, second, third, fourth)
 
+    loads = [
+        pltpu.make_async_copy(source, target, load_sem.at[at])
+        for at, (source, target) in enumerate(
+            ((u_hbm, u_ref), (bone_hbm, bone_ref), (words_hbm, words_ref), (v_hbm, v_ref))
+        )
+    ]
+    for load in loads:
+        load.start()
     barrier = pltpu.get_barrier_semaphore()
     expected = jnp.int32(0)
     for dx, dy in AROUND:
@@ -212,6 +222,8 @@
     for part in exchanges:
         part.packed[...] = jnp.zeros(part.packed.shape, part.packed.dtype)
         part.clear()
+    for load in loads:
+        load.wait()
     for axis in range(3):
         own1[axis] = u_ref[axis]
     own1[3] = bone_ref[...].astype(jnp.float32)
@@ -362,7 +374,8 @@
     tall = rows + 8
     copies = 4 * len(AROUND) + 5
     scratch = (
-        exchanged(4)
+        [pltpu.VMEM(array.shape, array.dtype) for array in (displacement, velocity, bone, broken)]
+        + exchanged(4)
         + [
             pltpu.VMEM((2, packed, depth), jnp.int32),
             pltpu.VMEM((1, words, layers, rows, depth), jnp.int32),
@@ -381,6 +394,7 @@
             floats(layers, rows, depth),
             pltpu.SemaphoreType.DMA((copies,)),
             pltpu.SemaphoreType.DMA((copies,)),
+            pltpu.SemaphoreType.DMA((4,)),
         ]
     )
     vmem = pl.BlockSpec(memory_space=pltpu.VMEM)
@@ -390,10 +404,12 @@
             jax.ShapeDtypeStruct(velocity.shape, jnp.float32),
             jax.ShapeDtypeStruct(bone.shape, jnp.float32),
         ),
-        in_specs=[vmem] * 4,
+        in_specs=[pl.BlockSpec(memory_space=pltpu.HBM)] * 4,
         out_specs=(vmem, vmem),
         scratch_shapes=scratch,
-        compiler_params=pltpu.CompilerParams(collective_id=0, has_side_effects=True),
+        compiler_params=pltpu.CompilerParams(
+            collective_id=0, has_side_effects=True, vmem_limit_bytes=VMEM_BYTES
+        ),
     )(displacement, velocity, bone, broken)
 
 

time: 32.7 us -> 31.9 us (0.976)
  Pallas kernels: 29.8 us -> 29 us
    pallas_call x1, Pallas kernels: 29.8 us -> 29 us  [body(): pl.pallas_call(functools.partial(kernel, count_x, count_y), out_shape=(ja...]
where the time goes in v1:
time: 31.9 us; the launch traced here: 31.7 us
  Pallas kernels  29 us (91%)
  local copies, waits for them, and re-layouts  2 us (6%)
  between operations  0.65 us (2%)
    pallas_call x1, Pallas kernels, body(): pl.pallas_call(functools.partial(kernel, count_x, count_y), out_shape=(ja...  29 us
    unnamed x4, local copies, waits for them, and re-layouts  2 us

profile of v1, /device:TPU:3, one launch (start us, length us, event | category | flops | bytes accessed | tf_op | source)
XLA Modules:
  0.0 31.7 jit_solution(2319846056195544850)
XLA Ops:
  0.6 29.0 %shard_map.59 = (f32[3,3,8,128]{3,2,1,0:T(8,128)}, f32[3,8,128]{2,1,0:T(8,128)}) custom-call(f32[3,3,8,128]{3,2,1,0:T(8,128)} %u_hbm.1, f32[3,3,8,128]{3,2,1,0:T(8,128)} %v_hbm.1, s32[3,8,128]{2,1,0:T(8,128)} %bone_hbm.1, s32[4,3,8,128]{3,2,1,0:T(8,128)} %words_hbm.1), custom_call_target="tpu_custom_call" | custom-call | tf_op jit(solution)/shard_map/pallas_call | solution.py:401
  29.7 0.0 copy-start
  29.7 1.4 %copy.8 = f32[3,3,8,128]{3,2,1,0:T(8,128)} copy(f32[3,3,8,128]{3,2,1,0:T(8,128)} %get-tuple-element.4) | data formatting | bytes 73728
  31.1 0.0 copy-done
  31.1 0.6 %copy.9 = f32[3,8,128]{2,1,0:T(8,128)} copy(f32[3,8,128]{2,1,0:T(8,128)S(1)} %copy-done) | data formatting | bytes 24576
Async XLA Ops:
  29.7 1.4 %copy-start = (f32[3,8,128]{2,1,0:T(8,128)S(1)}, f32[3,8,128]{2,1,0:T(8,128)}, u32[]{:S(2)}) copy-start(f32[3,8,128]{2,1,0:T(8,128)} %get-tuple-element.5) | copy-start | bytes 36868

commit v2 on v1

--- a/solution.py
+++ b/solution.py
@@ -101,14 +101,18 @@
                 slot[...] = jnp.zeros(slot.shape, slot.dtype)
 
     def start(self):
-        for number, (dx, dy) in enumerate(self.sides):
+        order = sorted(range(len(self.sides)), key=lambda at: (self.sides[at][0] != 0, self.sides[at][1] == 0))
+        for number in order:
+            dx, dy = self.sides[number]
 
             @pl.when(self.has(dx, dy))
             def _():
                 self.copy(number).start()
 
-    def wait_recv(self):
+    def wait_recv(self, remote):
         for number, (dx, dy) in enumerate(self.sides):
+            if (dx != 0) != remote:
+                continue
 
             @pl.when(self.has(-dx, -dy))
             def _():
@@ -140,10 +144,10 @@
                     ]
 
 
-def spread_rolls(rolled, fields, change=None):
-    layers, rows, depth = rolled.shape[2:]
-
-    @pl.loop(0, layers)
+def spread_rolls(rolled, fields, first, last, change=None):
+    rows, depth = rolled.shape[3:]
+
+    @pl.loop(first, last)
     def _(layer):
         for field in fields:
             for half in range(0, rows, 8):
@@ -167,7 +171,7 @@
     own2, pack2, fx2, fy2,
     own3, pack3, fx3, fy3,
     own4, pack4, fx4, fy4,
-    near, near_words, ratio, masks, pulls, stretches, volumes,
+    near, near_words, ratio, masks, weights, pulls, stretches, volumes, sums_ref, force_ref,
     send_sem, recv_sem, load_sem,
 ):
     place = (lax.axis_index("gx"), lax.axis_index("gy"))
@@ -243,68 +247,123 @@
             return jnp.where(inside, moved, 0.0)
         return moved
 
+    def bonds_of(layer, remote):
+        for number, bond in enumerate(bonds):
+            if (0 <= layer + bond[0] < layers) != remote:
+                yield (number,) + bond
+
+    def relative(moving, layer, here, step_x, step_y, step_z):
+        low = ROW + step_y
+        rel = []
+        for axis, step in enumerate((step_x, step_y, 0)):
+            far = near[REACH + step_z, axis, layer + layers + step_x, low : low + rows]
+            rel.append(far - (here[axis] - float(step)))
+        return rel, rel[0] * rel[0] + rel[1] * rel[1] + rel[2] * rel[2]
+
+    def put_pulls(number, layer, rel, squared, weight):
+        pull = weight * lax.rsqrt(squared + DIRECTION_EPS)
+        for axis in range(3):
+            pulls[number, axis, layer] = pull * rel[axis]
+
+    def strain(moving, opening, last_step, layer, remote):
+        here = [moving[axis, layer] for axis in range(3)]
+        total = sums_ref[0, layer] if remote else jnp.zeros((rows, depth), jnp.float32)
+        sums = {}
+        words_here = [words_ref[word, layer] for word in range(4)] if opening else None
+        for number, step_x, step_y, step_z, flag, backward in bonds_of(layer, remote):
+            low = ROW + step_y
+            rel, squared = relative(moving, layer, here, step_x, step_y, step_z)
+            length = squared * lax.rsqrt(jnp.maximum(squared, 1e-30))
+            norm = step_x * step_x + step_y * step_y + step_z * step_z
+            natural = math.sqrt(norm)
+            extension = length - natural
+            power = extension * (LOG2_E / (STRETCH_WIDTH * natural)) - (
+                STRETCH_CRITICAL * LOG2_E / STRETCH_WIDTH
+            )
+            if opening:
+                word, bit = flag_place(flag)
+                if backward:
+                    held = near_words[
+                        REACH + step_z, word, layer + layers + step_x, low : low + rows
+                    ]
+                else:
+                    held = words_here[word]
+                far_bone = near[REACH + step_z, 3, layer + layers + step_x, low : low + rows]
+                intact = jnp.where((held & (1 << bit)) == 0, far_bone, 0.0)
+                masks[number, layer] = intact
+                sums[norm] = sums[norm] + intact if norm in sums else intact
+            else:
+                intact = masks[number, layer]
+            weight = intact / (1.0 + jnp.exp2(power))
+            if last_step:
+                sums[norm] = sums[norm] + weight if norm in sums else weight
+            total = total + weight * extension
+            stretches[number, layer] = extension * (1.0 / natural)
+            if remote:
+                weights[number, layer] = weight
+            else:
+                put_pulls(number, layer, rel, squared, weight)
+        sums_ref[0, layer] = total
+        weighted = sums_ref[1, layer] if remote else jnp.zeros((rows, depth), jnp.float32)
+        for norm, value in sums.items():
+            weighted = weighted + value * math.sqrt(norm)
+        sums_ref[1, layer] = weighted
+
+    def direct(moving, layer):
+        here = [moving[axis, layer] for axis in range(3)]
+        for number, step_x, step_y, step_z, flag, backward in bonds_of(layer, True):
+            rel, squared = relative(moving, layer, here, step_x, step_y, step_z)
+            put_pulls(number, layer, rel, squared, weights[number, layer])
+
+    def push(ratios, layer, remote):
+        scaled = ratios.own[0, layer]
+        inverse = own2[1, layer]
+        if remote:
+            force = [force_ref[axis, layer] for axis in range(3)]
+        else:
+            force = [jnp.zeros((rows, depth), jnp.float32) for axis in range(3)]
+        for number, step_x, step_y, step_z, flag, backward in bonds_of(layer, remote):
+            low = ROW + step_y
+            far = [
+                ratio[REACH + step_z, kind, layer + layers + step_x, low : low + rows]
+                for kind in range(2)
+            ]
+            magnitude = (scaled + far[0]) + stretches[number, layer] * (inverse + far[1])
+            for axis in range(3):
+                force[axis] = force[axis] + magnitude * pulls[number, axis, layer]
+        if not remote:
+            for axis in range(3):
+                force_ref[axis, layer] = force[axis]
+        return force
+
+    def sides_of(remote):
+        if remote:
+            return (-1, 1), ((0, layers), (2 * layers, 3 * layers))
+        return (0,), ((layers, 2 * layers),)
+
     for step_index in range(STEPS):
         opening = step_index == 0
         last_step = step_index == STEPS - 1
         source = first if opening else third
-        source.wait_recv()
-        source.assemble(near.at[REACH], (-1, 0, 1))
-        spread_rolls(near, range(4 if opening else 3), shifted)
-        if opening:
-            flags.wait_recv()
-            flags.assemble(near_words.at[REACH], (-1, 0))
-            spread_rolls(near_words, range(4))
         moving = u_ref if opening else own3
         ratios = second if opening else fourth
-
-        @pl.loop(0, layers)
-        def _(layer):
-            here = [moving[axis, layer] for axis in range(3)]
-            total = jnp.zeros((rows, depth), jnp.float32)
-            sums = {}
+        for remote in (False, True):
+            dxs, spans = sides_of(remote)
+            source.wait_recv(remote)
+            source.assemble(near.at[REACH], dxs)
+            for low, high in spans:
+                spread_rolls(near, range(4 if opening else 3), low, high, shifted)
             if opening:
-                words_here = [words_ref[word, layer] for word in range(4)]
-            for number, (step_x, step_y, step_z, flag, backward) in enumerate(bonds):
-                low = ROW + step_y
-                rel = []
-                for axis, step in enumerate((step_x, step_y, 0)):
-                    far = near[REACH + step_z, axis, layer + layers + step_x, low : low + rows]
-                    rel.append(far - (here[axis] - float(step)))
-                squared = rel[0] * rel[0] + rel[1] * rel[1] + rel[2] * rel[2]
-                length = squared * lax.rsqrt(jnp.maximum(squared, 1e-30))
-                norm = step_x * step_x + step_y * step_y + step_z * step_z
-                natural = math.sqrt(norm)
-                extension = length - natural
-                power = extension * (LOG2_E / (STRETCH_WIDTH * natural)) - (
-                    STRETCH_CRITICAL * LOG2_E / STRETCH_WIDTH
-                )
-                if opening:
-                    word, bit = flag_place(flag)
-                    if backward:
-                        held = near_words[
-                            REACH + step_z, word, layer + layers + step_x, low : low + rows
-                        ]
-                    else:
-                        held = words_here[word]
-                    far_bone = near[REACH + step_z, 3, layer + layers + step_x, low : low + rows]
-                    intact = jnp.where((held & (1 << bit)) == 0, far_bone, 0.0)
-                    masks[number, layer] = intact
-                    sums[norm] = sums[norm] + intact if norm in sums else intact
-                else:
-                    intact = masks[number, layer]
-                weight = intact / (1.0 + jnp.exp2(power))
-                if last_step:
-                    sums[norm] = sums[norm] + weight if norm in sums else weight
-                total = total + weight * extension
-                stretches[number, layer] = extension * (1.0 / natural)
-                pull = weight * lax.rsqrt(squared + DIRECTION_EPS)
-                for axis in range(3):
-                    pulls[number, axis, layer] = pull * rel[axis]
+                flags.wait_recv(remote)
+                flags.assemble(near_words.at[REACH], dxs[:1])
+                spread_rolls(near_words, range(4), *spans[0])
+            for layer in range(layers):
+                strain(moving, opening, last_step, layer, remote)
+
+        for layer in range(layers):
+            total = sums_ref[0, layer]
             bone_here = own1[3, layer]
-            weighted = jnp.zeros((rows, depth), jnp.float32)
-            for norm, value in sums.items():
-                weighted = weighted + value * math.sqrt(norm)
-            weighted = weighted * bone_here
+            weighted = sums_ref[1, layer] * bone_here
             if opening:
                 volume = jnp.maximum(weighted, 1.0)
                 inverse = 1.0 / volume
@@ -319,31 +378,25 @@
 
         ratios.pack()
         ratios.start()
-        ratios.wait_recv()
-        ratios.assemble(ratio.at[REACH], (-1, 0, 1))
-        spread_rolls(ratio, range(2 if opening else 1))
-
-        @pl.loop(0, layers)
-        def _(layer):
-            scaled = ratios.own[0, layer]
-            inverse = own2[1, layer]
-            force = [jnp.zeros((rows, depth), jnp.float32) for axis in range(3)]
-            for number, (step_x, step_y, step_z, flag, backward) in enumerate(bonds):
-                low = ROW + step_y
-                far = [
-                    ratio[REACH + step_z, kind, layer + layers + step_x, low : low + rows]
-                    for kind in range(2)
-                ]
-                magnitude = (scaled + far[0]) + stretches[number, layer] * (inverse + far[1])
+        for layer in range(layers):
+            direct(moving, layer)
+        for remote in (False, True):
+            dxs, spans = sides_of(remote)
+            ratios.wait_recv(remote)
+            ratios.assemble(ratio.at[REACH], dxs)
+            for low, high in spans:
+                spread_rolls(ratio, range(2 if opening else 1), low, high)
+            for layer in range(layers):
+                force = push(ratios, layer, remote)
+                if not remote:
+                    continue
+                bone_here = own1[3, layer] * TIME_STEP
                 for axis in range(3):
-                    force[axis] = force[axis] + magnitude * pulls[number, axis, layer]
-            bone_here = own1[3, layer] * TIME_STEP
-            for axis in range(3):
-                before = v_ref[axis, layer] if opening else velocity_ref[axis, layer]
-                speed = before + force[axis] * bone_here
-                velocity_ref[axis, layer] = speed
-                if not last_step:
-                    own3[axis, layer] = u_ref[axis, layer] + TIME_STEP * speed
+                    before = v_ref[axis, layer] if opening else velocity_ref[axis, layer]
+                    speed = before + force[axis] * bone_here
+                    velocity_ref[axis, layer] = speed
+                    if not last_step:
+                        own3[axis, layer] = u_ref[axis, layer] + TIME_STEP * speed
 
         if not last_step:
             third.pack()
@@ -389,9 +442,12 @@
             pltpu.VMEM((2 * REACH + 1, words, 2 * layers, tall, depth), jnp.int32),
             floats(2 * REACH + 1, 2, 3 * layers, tall, depth),
             floats(bonds, layers, rows, depth),
+            floats(bonds, layers, rows, depth),
             floats(bonds, 3, layers, rows, depth),
             floats(bonds, layers, rows, depth),
             floats(layers, rows, depth),
+            floats(2, layers, rows, depth),
+            floats(3, layers, rows, depth),
             pltpu.SemaphoreType.DMA((copies,)),
             pltpu.SemaphoreType.DMA((copies,)),
             pltpu.SemaphoreType.DMA((4,)),

time: 31.9 us -> 28.6 us (0.90)
  Pallas kernels: 29 us -> 25.4 us
    pallas_call x1, Pallas kernels: 29 us -> 25.4 us  [body(): pl.pallas_call(functools.partial(kernel, count_x, count_y), out_shape=(ja...]
where the time goes in v2:
time: 28.6 us; the launch traced here: 28.1 us
  Pallas kernels  25.4 us (89%)
  local copies, waits for them, and re-layouts  2 us (7%)
  between operations  0.65 us (2%)
    pallas_call x1, Pallas kernels, body(): pl.pallas_call(functools.partial(kernel, count_x, count_y), out_shape=(ja...  25.4 us
    unnamed x4, local copies, waits for them, and re-layouts  2 us

profile of v2, /device:TPU:3, one launch (start us, length us, event | category | flops | bytes accessed | tf_op | source)
XLA Modules:
  0.0 28.1 jit_solution(7553879561236688473)
XLA Ops:
  0.6 25.4 %shard_map.59 = (f32[3,3,8,128]{3,2,1,0:T(8,128)}, f32[3,8,128]{2,1,0:T(8,128)}) custom-call(f32[3,3,8,128]{3,2,1,0:T(8,128)} %u_hbm.1, f32[3,3,8,128]{3,2,1,0:T(8,128)} %v_hbm.1, s32[3,8,128]{2,1,0:T(8,128)} %bone_hbm.1, s32[4,3,8,128]{3,2,1,0:T(8,128)} %words_hbm.1), custom_call_target="tpu_custom_call" | custom-call | tf_op jit(solution)/shard_map/pallas_call | solution.py:457
  26.1 0.0 copy-start
  26.1 1.4 %copy.8 = f32[3,3,8,128]{3,2,1,0:T(8,128)} copy(f32[3,3,8,128]{3,2,1,0:T(8,128)} %get-tuple-element.4) | data formatting | bytes 73728
  27.5 0.0 copy-done
  27.5 0.6 %copy.9 = f32[3,8,128]{2,1,0:T(8,128)} copy(f32[3,8,128]{2,1,0:T(8,128)S(1)} %copy-done) | data formatting | bytes 24576
Async XLA Ops:
  26.1 1.4 %copy-start = (f32[3,8,128]{2,1,0:T(8,128)S(1)}, f32[3,8,128]{2,1,0:T(8,128)}, u32[]{:S(2)}) copy-start(f32[3,8,128]{2,1,0:T(8,128)} %get-tuple-element.5) | copy-start | bytes 36868

commit v3 on v2

--- a/solution.py
+++ b/solution.py
@@ -144,7 +144,7 @@
                     ]
 
 
-def spread_rolls(rolled, fields, first, last, change=None):
+def spread_rolls(rolled, fields, first, last, reach, change=None):
     rows, depth = rolled.shape[3:]
 
     @pl.loop(first, last)
@@ -152,7 +152,7 @@
         for field in fields:
             for half in range(0, rows, 8):
                 tile = rolled[REACH, field, layer, half : half + 8]
-                for step_z in range(-REACH, REACH + 1):
+                for step_z in range(-reach, reach + 1):
                     if step_z == 0:
                         continue
                     moved = pltpu.roll(tile, (-step_z) % depth, 1)
@@ -338,8 +338,9 @@
 
     def sides_of(remote):
         if remote:
-            return (-1, 1), ((0, layers), (2 * layers, 3 * layers))
-        return (0,), ((layers, 2 * layers),)
+            spans = ((layers - REACH + 1, layers), (2 * layers, 2 * layers + REACH - 1))
+            return (-1, 1), spans, REACH - 1
+        return (0,), ((layers, 2 * layers),), REACH
 
     for step_index in range(STEPS):
         opening = step_index == 0
@@ -348,15 +349,15 @@
         moving = u_ref if opening else own3
         ratios = second if opening else fourth
         for remote in (False, True):
-            dxs, spans = sides_of(remote)
+            dxs, spans, reach = sides_of(remote)
             source.wait_recv(remote)
             source.assemble(near.at[REACH], dxs)
             for low, high in spans:
-                spread_rolls(near, range(4 if opening else 3), low, high, shifted)
+                spread_rolls(near, range(4 if opening else 3), low, high, reach, shifted)
             if opening:
                 flags.wait_recv(remote)
                 flags.assemble(near_words.at[REACH], dxs[:1])
-                spread_rolls(near_words, range(4), *spans[0])
+                spread_rolls(near_words, range(4), *spans[0], reach)
             for layer in range(layers):
                 strain(moving, opening, last_step, layer, remote)
 
@@ -381,11 +382,11 @@
         for layer in range(layers):
             direct(moving, layer)
         for remote in (False, True):
-            dxs, spans = sides_of(remote)
+            dxs, spans, reach = sides_of(remote)
             ratios.wait_recv(remote)
             ratios.assemble(ratio.at[REACH], dxs)
             for low, high in spans:
-                spread_rolls(ratio, range(2 if opening else 1), low, high)
+                spread_rolls(ratio, range(2 if opening else 1), low, high, reach)
             for layer in range(layers):
                 force = push(ratios, layer, remote)
                 if not remote:

time: 28.6 us -> 27.5 us (0.962)
  the two profiles are of different devices: /device:TPU:3 before, /device:TPU:1 now
where the time goes in v3:
time: 27.5 us; the launch traced here: 27.3 us
  Pallas kernels  24.6 us (89%)
  local copies, waits for them, and re-layouts  2 us (7%)
  between operations  0.65 us (2%)
    pallas_call x1, Pallas kernels, body(): pl.pallas_call(functools.partial(kernel, count_x, count_y), out_shape=(ja...  24.6 us
    unnamed x4, local copies, waits for them, and re-layouts  2 us

profile of v3, /device:TPU:1, one launch (start us, length us, event | category | flops | bytes accessed | tf_op | source)
XLA Modules:
  0.0 27.3 jit_solution(17781374157379711236)
XLA Ops:
  0.6 24.6 %shard_map.59 = (f32[3,3,8,128]{3,2,1,0:T(8,128)}, f32[3,8,128]{2,1,0:T(8,128)}) custom-call(f32[3,3,8,128]{3,2,1,0:T(8,128)} %u_hbm.1, f32[3,3,8,128]{3,2,1,0:T(8,128)} %v_hbm.1, s32[3,8,128]{2,1,0:T(8,128)} %bone_hbm.1, s32[4,3,8,128]{3,2,1,0:T(8,128)} %words_hbm.1), custom_call_target="tpu_custom_call" | custom-call | tf_op jit(solution)/shard_map/pallas_call | solution.py:458
  25.3 0.0 copy-start
  25.3 1.4 %copy.8 = f32[3,3,8,128]{3,2,1,0:T(8,128)} copy(f32[3,3,8,128]{3,2,1,0:T(8,128)} %get-tuple-element.4) | data formatting | bytes 73728
  26.7 0.0 copy-done
  26.7 0.6 %copy.9 = f32[3,8,128]{2,1,0:T(8,128)} copy(f32[3,8,128]{2,1,0:T(8,128)S(1)} %copy-done) | data formatting | bytes 24576
Async XLA Ops:
  25.3 1.4 %copy-start = (f32[3,8,128]{2,1,0:T(8,128)S(1)}, f32[3,8,128]{2,1,0:T(8,128)}, u32[]{:S(2)}) copy-start(f32[3,8,128]{2,1,0:T(8,128)} %get-tuple-element.5) | copy-start | bytes 36868
